TPU v7x, 512 devices: a whole 4x4x16 slice. The times are simulated.
512 devices in a mesh: seq: 64 (over y_lo, z, core), kv: 8 (over x, y_hi).
Axes of the slice: x: 4, y: 4 (y_hi: 2, y_lo: 2; y = y_hi * 2 + y_lo), z: 16, core: 2. Of those that a mesh axis runs over, the one named last changes fastest.
Arguments:
- queries: bfloat16 [64, 16384, 128], P('kv', 'seq'), may hold values from -56 to 56
- key_states: bfloat16 [8, 16384, 128], P('kv', 'seq'), may hold values from -56 to 56
- samples: int32 [64, 512], P('kv', 'seq'), may hold values from 0 to 16383, as said below
- query_gate_weight: float32 [128, 128], replicated, may hold values from -6 to 6
- key_gate_weight: float32 [384, 128], replicated, may hold values from -0.3125 to 0.3125
Outputs:
- row_loss: float32 [64, 512], P('kv', 'seq')
- query_grad: float32 [128, 128], replicated
- key_grad: float32 [384, 128], replicated
Inputs may be any that keep to these rules, and one draw needn't show every extreme that they name: `samples`: sampled row r of every head lies in the tokens r // 8 * 256 to (r // 8 + 1) * 256 - 1; positions may repeat.
All inputs are finite; a program needn't handle non-finite values.
Results may differ from a plain program's by a relative error of at most 0.0003.
Values may be sent and summed in bfloat16 or wider, within the bound.
A program may use at most 64 MiB of HBM per device.

v0:
```python
import math
import jax
import jax.numpy as jnp
from jax import lax
from jax.sharding import Mesh
from jax.sharding import PartitionSpec as P

BLOCK = 128
SEQ = ("seq_0", "seq_1", "seq_2")
SEQ_KV = ("seq_0", "seq_1", "seq_2", "kv")
masked_score = -1e30
highest = lax.Precision.HIGHEST


def laid_out(tiles, dim):
    shape = list(tiles.shape[1:])
    shape[dim] *= tiles.shape[0]
    return jnp.moveaxis(tiles, 0, dim).reshape(shape)


def gather_in_order(array, axes, sequence):
    tiles = array[None]
    for k in sequence:
        tiles = lax.all_gather(tiles, axes[k], axis=0, tiled=True)
    held = [lax.axis_size(axes[k]) for k in reversed(sequence)]
    tiles = tiles.reshape(*held, *array.shape)
    turned = sorted(range(len(sequence)), key=lambda place: sequence[len(sequence) - 1 - place])
    return tiles.transpose(*turned, *range(len(sequence), tiles.ndim)).reshape(-1, *array.shape)


def gathered_by_axis(array, axes, sequence, dim):
    return laid_out(gather_in_order(array, axes, sequence), dim)


def from_everyone(array, axis):
    copies = jnp.broadcast_to(array, (lax.axis_size(axis), *array.shape))
    return lax.all_to_all(copies, axis, split_axis=0, concat_axis=0, tiled=True)


def gather_directly(array, axis, dim):
    return laid_out(from_everyone(array, axis), dim)


def in_blocks(array, dim, peers):
    shape = array.shape
    tiles = array.reshape(*shape[:dim], peers, shape[dim] // peers, *shape[dim + 1 :])
    return jnp.moveaxis(tiles, dim, 0)


def sent_and_summed(array, axis, dim):
    tiles = in_blocks(array, dim, lax.axis_size(axis))
    arrived = lax.all_to_all(tiles, axis, split_axis=0, concat_axis=0, tiled=True)
    return arrived.sum(axis=0)


def in_one(arrays, axis):
    ends = [0]
    for a in arrays:
        ends.append(ends[-1] + a.size)
    so_far = lax.psum(jnp.concatenate([a.ravel() for a in arrays]), axis)
    return tuple((so_far[b:e].reshape(a.shape) for a, b, e in zip(arrays, ends, ends[1:])))


def score_tile(row_block, key_block):
    return lax.dot_general(
        row_block, key_block, (((1,), (1,)), ((), ())), preferred_element_type=jnp.float32
    )


def body(queries, key_states, samples, query_gate_weight, key_gate_weight):
    head_count, shard_len, head_width = queries.shape
    rows_local = samples.shape[1]
    gate_width = query_gate_weight.shape[1]
    seq_devices = lax.axis_size(SEQ)
    shard_index = lax.axis_index(SEQ)
    offset = shard_index * shard_len
    local_blocks = shard_len // BLOCK
    total_blocks = local_blocks * seq_devices
    score_scale = 1.0 / math.sqrt(head_width)
    gate_scale = 1.0 / math.sqrt(gate_width)
    pooled_query = jnp.mean(
        queries.reshape(head_count, local_blocks, BLOCK, head_width), axis=2, dtype=jnp.float32
    )
    key_rows = key_states[0]
    key_blocks = key_rows.reshape(local_blocks, BLOCK, head_width)
    pooled_key = jnp.concatenate(
        [
            jnp.max(key_blocks, axis=1).astype(jnp.float32),
            jnp.min(key_blocks, axis=1).astype(jnp.float32),
            jnp.mean(key_blocks, axis=1, dtype=jnp.float32),
        ],
        axis=-1,
    )
    gate_key = jnp.dot(pooled_key, key_gate_weight, precision=highest)
    local_places = samples - offset
    query_rows = jnp.take_along_axis(queries, local_places[:, :, None], axis=1)
    row_count = head_count * rows_local
    flat_rows = query_rows.reshape(row_count, head_width)
    flat_places = samples.reshape(row_count)
    initial = (
        jnp.full((row_count,), masked_score, jnp.float32),
        jnp.zeros((row_count, total_blocks), jnp.float32),
    )
    pieces = gathered_by_axis(key_rows, SEQ, (0, 1, 2), 0).reshape(-1, shard_len, head_width)

    def absorb_one(turn_number, running):
        running_top, running_mass = running
        first_key = turn_number * shard_len
        scores = score_tile(flat_rows, pieces[turn_number]) * score_scale
        causal = (first_key + jnp.arange(shard_len, dtype=jnp.int32))[None, :] <= flat_places[
            :, None
        ]
        tile_top = jnp.max(jnp.where(causal, scores, masked_score), axis=1)
        new_top = jnp.maximum(running_top, tile_top)
        weights = jnp.where(causal, jnp.exp(scores - new_top[:, None]), 0.0)
        tile_mass = jnp.sum(weights.reshape(row_count, local_blocks, BLOCK), axis=2)
        rescaled = running_mass * jnp.exp(running_top - new_top)[:, None]
        placed = lax.dynamic_update_slice(rescaled, tile_mass, (jnp.int32(0), first_key // BLOCK))
        return (new_top, placed)

    running_top, running_mass = lax.fori_loop(0, pieces.shape[0], absorb_one, initial)
    teacher = running_mass / jnp.sum(running_mass, axis=1, keepdims=True)
    every_key = gather_directly(gate_key, SEQ, 0)
    gate_query = jnp.einsum("hcd,dg->hcg", pooled_query, query_gate_weight, precision=highest)
    local_block = local_places // BLOCK
    gate_rows = jnp.take_along_axis(gate_query, local_block[:, :, None], axis=1).reshape(
        row_count, gate_width
    )
    pooled_rows = jnp.take_along_axis(pooled_query, local_block[:, :, None], axis=1).reshape(
        row_count, head_width
    )
    own_block = flat_places // BLOCK
    allowed = jnp.arange(total_blocks, dtype=jnp.int32)[None, :] <= own_block[:, None]
    logits = jnp.dot(gate_rows, every_key.T, precision=highest) * gate_scale
    logit_top = jnp.max(jnp.where(allowed, logits, masked_score), axis=1)
    gate_weights = jnp.where(allowed, jnp.exp(logits - logit_top[:, None]), 0.0)
    gate_total = jnp.sum(gate_weights, axis=1)
    log_total = logit_top + jnp.log(gate_total)
    flat_loss = log_total - jnp.sum(jnp.where(allowed, teacher * logits, 0.0), axis=1)
    gate_delta = jnp.where(allowed, gate_weights / gate_total[:, None] - teacher, 0.0)
    query_part = jnp.dot(
        pooled_rows.T,
        jnp.dot(gate_delta, every_key, precision=highest) * gate_scale,
        precision=highest,
    )
    key_delta = sent_and_summed(
        jnp.dot(gate_delta.T, gate_rows, precision=highest) * gate_scale, SEQ, 0
    )
    key_part = jnp.dot(pooled_key.T, key_delta, precision=highest)
    row_loss = flat_loss.reshape(head_count, rows_local)
    query_grad, key_grad = in_one((query_part, key_part), SEQ_KV)
    return (row_loss, query_grad, key_grad)


def solution(mesh):
    torus = Mesh(
        mesh.devices.reshape(2, 16, 2, mesh.shape["kv"]), ("seq_0", "seq_1", "seq_2", "kv")
    )
    placed = (P("kv", SEQ, None), P("kv", SEQ, None), P("kv", SEQ), P(), P())
    return jax.shard_map(
        body, mesh=torus, in_specs=placed, out_specs=(P("kv", SEQ), P(), P()), check_vma=False
    )
```

profile of v0, /device:TPU:2, one launch (start us, length us, event | category | flops | bytes accessed | tf_op | source)
XLA Modules:
  0.0 741.4 jit_solution(1190638927435643087)
XLA Ops:
  7.2 6.4 all_gather.9
  13.7 76.9 %all-gather.3.cloned.1.call-done = bf16[32,256,128]{2,1,0:T(8,128)(2,1)} async-done(((bf16[2,256,128]{2,1,0:T(8,128)(2,1)}), bf16[32,256,128]{2,1,0:T(8,128)(2,1)}) %all-gather.3.cloned.1.call-update) | async-done | bytes 2097168 | tf_op jit(solution)/shard_map/all_gather | solution.py:24
  93.3 9.6 %all-to-all-start = ((f32[64,2,128]{2,1,0:T(2,128)}), f32[64,2,128]{2,1,0:T(2,128)S(1)}, u32[]{:S(2)}, u32[]{:S(2)}) async-start(f32[64,2,128]{2,1,0:T(2,128)} %broadcast_in_dim.73), calls=%async_computation | async-start | bytes 131072 | tf_op jit(solution)/shard_map/all_to_all | solution.py:37
  103.6 1.1 convert_reduce_fusion
  110.5 1.7 gather_fusion
  112.3 5.1 all-to-all-done
  117.8 4.7 copy.13
  122.4 125.2 %while.19 = (s32[]{:T(128)}, f32[64]{0:T(128)S(1)}, f32[64,128]{1,0:T(8,128)S(1)}, s32[8,8]{1,0:T(8,128)}, bf16[64,256,128]{2,1,0:T(8,128)(2,1)}, /*index=5*/bf1...) while((s32[]{:T(128)}, f32[64]{0:T(128)S(1)}, ...), condition=%wide.wide.region_9.11_spmd.clone, body=%wide.wide.region_6.10_spmd.clone.sunk | while | flops 4333846 | bytes 548455 | solution.py:121
  130.1 1.1 fusion.39
  136.0 1.1 fusion.39
  145.8 1.1 fusion.39
  151.7 1.1 fusion.39
  157.5 1.1 fusion.39
  167.3 1.1 fusion.39
  173.2 1.1 fusion.39
  183.0 1.1 fusion.39
  188.9 1.1 fusion.39
  194.8 1.1 fusion.39
  204.6 1.1 fusion.39
  248.9 10.0 %all-to-all-start.1 = ((f32[64,2,128]{2,1,0:T(2,128)}), f32[64,2,128]{2,1,0:T(2,128)S(1)}, u32[]{:S(2)}, u32[]{:S(2)}) async-start(f32[64,2,128]{2,1,0:T(2,128)} %bitcast.16), calls=%async_computation.1 | async-start | bytes 131072 | tf_op jit(solution)/shard_map/all_to_all | solution.py:52
  259.7 13.8 %all-to-all-done.1 = f32[64,2,128]{2,1,0:T(2,128)S(1)} async-done(((f32[64,2,128]{2,1,0:T(2,128)}), f32[64,2,128]{2,1,0:T(2,128)S(1)}, u32[]{:S(2)}, u32[]{:S(2)}) %all-to-all-start.1) | async-done | bytes 65568 | tf_op jit(solution)/shard_map/all_to_all | solution.py:52
  275.5 456.2 %all-reduce.2.cloned.1.call-done = f32[65536]{0:T(1024)} async-done(((f32[65536]{0:T(1024)}), f32[65536]{0:T(1024)}) %all-reduce.2.cloned.1.call-update) | async-done | bytes 262160 | tf_op jit(solution)/shard_map/psum | solution.py:60
  731.7 1.6 slice_bitcast_fusion
  733.4 1.5 slice_bitcast_fusion.1
  (545 shorter events, 120.9 us)
Async XLA Ops:
  7.2 85.2 %copy-start = (f32[384,128]{1,0:T(8,128)S(1)}, f32[384,128]{1,0:T(8,128)}, u32[]{:S(2)}) copy-start(f32[384,128]{1,0:T(8,128)} %param.13) | copy-start | bytes 589828
  7.2 83.4 %all-gather.3.cloned.1.call-start = ((), (), s32[]{:S(2)}) async-start(), calls=%async_computation.2 | async-start | bytes 2228224 | tf_op jit(solution)/shard_map/all_gather | solution.py:24
  13.6 104.1 %all-gather.5.cloned.1.call-start = ((), (), s32[]{:S(2)}) async-start(), calls=%async_computation.3 | async-start | bytes 6291456 | tf_op jit(solution)/shard_map/all_gather | solution.py:24
  93.3 24.1 %all-to-all-start = ((f32[64,2,128]{2,1,0:T(2,128)}), f32[64,2,128]{2,1,0:T(2,128)S(1)}, u32[]{:S(2)}, u32[]{:S(2)}) async-start(f32[64,2,128]{2,1,0:T(2,128)} %broadcast_in_dim.73), calls=%async_computation | async-start | bytes 131072 | tf_op jit(solution)/shard_map/all_to_all | solution.py:37
  248.9 24.6 %all-to-all-start.1 = ((f32[64,2,128]{2,1,0:T(2,128)}), f32[64,2,128]{2,1,0:T(2,128)S(1)}, u32[]{:S(2)}, u32[]{:S(2)}) async-start(f32[64,2,128]{2,1,0:T(2,128)} %bitcast.16), calls=%async_computation.1 | async-start | bytes 131072 | tf_op jit(solution)/shard_map/all_to_all | solution.py:52
  259.0 472.7 %all-reduce.2.cloned.1.call-start = ((), (), s32[]{:S(2)}) async-start(), calls=%async_computation.4 | async-start | bytes 524288 | tf_op jit(solution)/shard_map/psum | solution.py:60
Sparse Core Ops, SparseCore 0:
  13.7 76.7 all-gather.2
  92.6 21.0 all-gather.4
  274.9 456.7 all-reduce.1
where the time goes:
time: 745 us; the launch traced here: 741 us
  waiting for transfers between devices  552 us (74%)
  matrix products  74.3 us (10%)
  local copies, waits for them, and re-layouts  42.7 us (6%)
  other arithmetic  26.4 us (4%)
  starting transfers between devices  19.8 us (3%)
  between operations  13.9 us (2%)
    psum x1, waiting for transfers between devices, in_one(): so_far = lax.psum(jnp.concatenate([a.ravel() for a in arrays]), axis)  456 us
    all_gather x2, waiting for transfers between devices, gather_in_order(): tiles = lax.all_gather(tiles, axes[k], axis=0, tiled=True)  76.9 us
    dot_general x64, matrix products, score_tile(): lax.dot_general(row_block, key_block, (((1,), (1,)), ((), ())), preferred...  70.5 us
    dynamic_update_slice x64, local copies, waits for them, and re-layouts, absorb_one(): lax.dynamic_update_slice(rescaled, tile_mass, (jnp.int32(0), first_key //...  26.3 us
  transfers between devices with their start and end apart: 5, of which 4 were waited for; matrix products, arithmetic and copies ran while one was open for 2% of the time, Pallas kernels for 0%

commit v1 on v0

--- a/solution.py
+++ b/solution.py
@@ -21,7 +21,10 @@
 def gather_in_order(array, axes, sequence):
     tiles = array[None]
     for k in sequence:
-        tiles = lax.all_gather(tiles, axes[k], axis=0, tiled=True)
+        peers_2 = lax.axis_size(axes[k])
+        blocks = jnp.stack([tiles for _ in range(peers_2)])
+        blocks = lax.all_to_all(blocks, axes[k], split_axis=0, concat_axis=0)
+        tiles = jnp.concatenate(blocks, axis=0)
     held = [lax.axis_size(axes[k]) for k in reversed(sequence)]
     tiles = tiles.reshape(*held, *array.shape)
     turned = sorted(range(len(sequence)), key=lambda place: sequence[len(sequence) - 1 - place])

time: 745 us -> 780 us (1.047)
  blocking collectives: 6.37 us -> 37.5 us
  waiting for transfers between devices: 552 us -> 562 us
    all_to_all x1 -> x2, waiting for transfers between devices: 5.06 us -> 91.6 us  [gather_in_order(): blocks = lax.all_to_all(blocks, axes[k], split_axis=0, concat_axis=0)]
    all_gather x2 -> x0, waiting for transfers between devices: 76.9 us -> none  [gather_in_order(): tiles = lax.all_gather(tiles, axes[k], axis=0, tiled=True)]
    all_to_all x0 -> x2, blocking collectives: none -> 37.5 us  [the longest x1 30.4 us: from_everyone(): return lax.all_to_all(copies, axis, split_axis=0, concat_axis=0, tiled=True)]
  transfers between devices with their start and end apart: 5 -> 4, of which waited for: 4 -> 4; matrix products, arithmetic and copies ran while one was open for 2% -> 1% of each run, Pallas kernels for 0% -> 0%
where the time goes in v1:
time: 780 us; the launch traced here: 776 us
  waiting for transfers between devices  562 us (72%)
  matrix products  73.4 us (9%)
  local copies, waits for them, and re-layouts  39.2 us (5%)
  blocking collectives  37.5 us (5%)
  other arithmetic  25.2 us (3%)
  starting transfers between devices  18.5 us (2%)
  between operations  14.2 us (2%)
    psum x1, waiting for transfers between devices, in_one(): so_far = lax.psum(jnp.concatenate([a.ravel() for a in arrays]), axis)  457 us
    all_to_all x2, waiting for transfers between devices, gather_in_order(): blocks = lax.all_to_all(blocks, axes[k], split_axis=0, concat_axis=0)  91.6 us
    dot_general x64, matrix products, score_tile(): lax.dot_general(row_block, key_block, (((1,), (1,)), ((), ())), preferred...  70.6 us
    all_to_all x1, blocking collectives, from_everyone(): return lax.all_to_all(copies, axis, split_axis=0, concat_axis=0, tiled=True)  30.4 us
    dynamic_update_slice x64, local copies, waits for them, and re-layouts, absorb_one(): lax.dynamic_update_slice(rescaled, tile_mass, (jnp.int32(0), first_key //...  26.3 us
  transfers between devices with their start and end apart: 4, of which 4 were waited for; matrix products, arithmetic and copies ran while one was open for 1% of the time, Pallas kernels for 0%

profile of v1, /device:TPU:2, one launch (start us, length us, event | category | flops | bytes accessed | tf_op | source)
XLA Modules:
  0.0 776.2 jit_solution(2521202650976112621)
XLA Ops:
  7.2 1.6 pad_maximum_fusion.2
  8.8 3.4 all-to-all-start.1
  14.2 2.5 all-to-all-done.1
  16.7 30.4 %all_to_all.25 = f32[64,2,128]{2,1,0:T(2,128)S(1)} all-to-all(f32[64,2,128]{2,1,0:T(2,128)S(1)} %broadcast_in_dim.73), channel_id=1, replica_groups=mesh['seq_0'=2,'seq_1'=16,'seq_2'=2,'kv'=8] {'seq_0','seq_1','seq_2'}, dimensions={0} | all-to-all | bytes 131072 | tf_op jit(solution)/shard_map/all_to_all | solution.py:40
  47.1 1.8 stack.10
  48.9 3.7 all-to-all-start.2
  56.3 89.1 %all-to-all-done.2 = bf16[16,2,256,128]{3,2,1,0:T(8,128)(2,1)S(1)} async-done(((bf16[16,2,256,128]{3,2,1,0:T(8,128)(2,1)}), bf16[16,2,256,128]{3,2,1,0:T(8,128)(2,1)S(1)}, u32[]{:S(2)}, u32[]{:S(2)}) %all-to-all-start.2) | async-done | bytes 2097184 | tf_op jit(solution)/shard_map/all_to_all | solution.py:26
  145.8 7.1 all_to_all.26
  152.9 2.2 copy.14
  155.1 125.1 %while.19 = (s32[]{:T(128)}, f32[64]{0:T(128)S(1)}, f32[64,128]{1,0:T(8,128)S(1)}, s32[8,8]{1,0:T(8,128)}, bf16[64,256,128]{2,1,0:T(8,128)(2,1)}, /*index=5*/bf1...) while((s32[]{:T(128)}, f32[64]{0:T(128)S(1)}, ...), condition=%wide.wide.region_9.11_spmd.clone, body=%wide.wide.region_6.10_spmd.clone.sunk | while | flops 4333846 | bytes 548455 | solution.py:124
  156.9 1.1 fusion.39
  158.9 1.1 fusion.39
  160.8 1.1 fusion.39
  162.8 1.1 fusion.39
  164.7 1.1 fusion.39
  166.7 1.1 fusion.39
  168.7 1.1 fusion.39
  170.6 1.1 fusion.39
  172.6 1.1 fusion.39
  281.6 11.4 %all-to-all-start.4 = ((f32[64,2,128]{2,1,0:T(2,128)}), f32[64,2,128]{2,1,0:T(2,128)S(1)}, u32[]{:S(2)}, u32[]{:S(2)}) async-start(f32[64,2,128]{2,1,0:T(2,128)} %bitcast.19), calls=%async_computation.4 | async-start | bytes 131072 | tf_op jit(solution)/shard_map/all_to_all | solution.py:55
  293.7 13.8 %all-to-all-done.4 = f32[64,2,128]{2,1,0:T(2,128)S(1)} async-done(((f32[64,2,128]{2,1,0:T(2,128)}), f32[64,2,128]{2,1,0:T(2,128)S(1)}, u32[]{:S(2)}, u32[]{:S(2)}) %all-to-all-start.4) | async-done | bytes 65568 | tf_op jit(solution)/shard_map/all_to_all | solution.py:55
  309.5 456.7 %all-reduce.2.cloned.1.call-done = f32[65536]{0:T(1024)} async-done(((f32[65536]{0:T(1024)}), f32[65536]{0:T(1024)}) %all-reduce.2.cloned.1.call-update) | async-done | bytes 262160 | tf_op jit(solution)/shard_map/psum | solution.py:63
  766.2 1.6 slice_bitcast_fusion
  767.9 1.5 slice_bitcast_fusion.1
  (551 shorter events, 119.2 us)
Async XLA Ops:
  7.2 6.8 copy-start
  7.2 45.5 %copy-start.2 = (s32[8,8]{1,0:T(8,128)S(1)}, s32[8,8]{1,0:T(8,128)}, u32[]{:S(2)}) copy-start(s32[8,8]{1,0:T(8,128)} %param.11) | copy-start | bytes 772
  7.2 45.7 %copy-start.1 = (bf16[8,256,128]{2,1,0:T(8,128)(2,1)S(1)}, bf16[8,256,128]{2,1,0:T(8,128)(2,1)}, u32[]{:S(2)}) copy-start(bf16[8,256,128]{2,1,0:T(8,128)(2,1)} %param.9) | copy-start | bytes 1572868
  7.2 45.8 %copy-start.3 = (f32[128,128]{1,0:T(8,128)S(1)}, f32[128,128]{1,0:T(8,128)}, u32[]{:S(2)}) copy-start(f32[128,128]{1,0:T(8,128)} %param.12) | copy-start | bytes 196612
  8.8 7.8 %all-to-all-start.1 = ((bf16[2,1,256,128]{3,2,1,0:T(8,128)(2,1)}), bf16[2,1,256,128]{3,2,1,0:T(8,128)(2,1)S(1)}, u32[]{:S(2)}, u32[]{:S(2)}) async-start(bf16[2,1,256,128]{3,2,1,0:T(8,128)(2,1)} %pad_maximum_fusion.2), calls=%async_computation.1 | async-start | bytes 262144 | tf_op jit(solution)/shard_map/all_to_all | solution.py:26
  48.9 96.5 %all-to-all-start.2 = ((bf16[16,2,256,128]{3,2,1,0:T(8,128)(2,1)}), bf16[16,2,256,128]{3,2,1,0:T(8,128)(2,1)S(1)}, u32[]{:S(2)}, u32[]{:S(2)}) async-start(bf16[16,2,256,128]{3,2,1,0:T(8,128)(2,1)} %stack.10), calls=%async_computation.2 | async-start | bytes 4194304 | tf_op jit(solution)/shard_map/all_to_all | solution.py:26
  281.6 25.9 %all-to-all-start.4 = ((f32[64,2,128]{2,1,0:T(2,128)}), f32[64,2,128]{2,1,0:T(2,128)S(1)}, u32[]{:S(2)}, u32[]{:S(2)}) async-start(f32[64,2,128]{2,1,0:T(2,128)} %bitcast.19), calls=%async_computation.4 | async-start | bytes 131072 | tf_op jit(solution)/shard_map/all_to_all | solution.py:55
  293.0 473.2 %all-reduce.2.cloned.1.call-start = ((), (), s32[]{:S(2)}) async-start(), calls=%async_computation.5 | async-start | bytes 524288 | tf_op jit(solution)/shard_map/psum | solution.py:63
Sparse Core Ops, SparseCore 0:
  309.0 457.2 all-reduce.1
